TPU v7x, 128 devices: a whole 4x4x4 slice. The times are simulated.
128 devices in a mesh: ctx: 16 (over x, z), head: 8 (over y, core).
Axes of the slice: x: 4, y: 4, z: 4, core: 2. Of those that a mesh axis runs over, the one named last changes fastest.
Arguments:
- queries: bfloat16 [8192, 8192], P(('ctx', 'head')), may hold values from -5 to 5
- keys: bfloat16 [8192, 1024], P(('ctx', 'head')), may hold values from -5 to 5
- values: bfloat16 [8192, 1024], P(('ctx', 'head')), may hold values from -6 to 6
- vert_blocks: int32 [8, 8], P('head'), may hold values from 0 to 47, as said below
Outputs:
- attended: bfloat16 [8192, 8192], P(('ctx', 'head'))
Inputs may be any that keep to these rules, and one draw needn't show every extreme that they name: `vert_blocks`: each row names 8 different blocks in rising order; the first is always block 0; the block (6144) // 128 - 1 appears in row 0.
All inputs are finite; a program needn't handle non-finite values.
Results may differ from a plain program's by a relative error of at most 0.0043.
Values may be sent and summed in bfloat16 or wider, within the bound.
A program may use at most 128 MiB of HBM per device.

v0:
```python
import math

import jax
import jax.numpy as jnp
from jax import lax
from jax.sharding import PartitionSpec as P

H = 64
KVH = 8
DH = 128
BAND = 2048
VW = 128
NV = 1024
QBLK = 512


def shifted(shard, axis, by):
    length = lax.axis_size(axis)
    pairs = [(i, i + by) for i in range(length) if 0 <= i + by < length]
    return lax.ppermute(shard, axis, pairs)


def select_rows(source, positions, anchor):
    count = source.shape[1]
    local = positions - anchor
    valid = (local >= 0) & (local < count)
    clipped = jnp.clip(local, 0, count - 1)
    head_index = jnp.arange(positions.shape[0], dtype=jnp.int32)[:, None]
    picked = source[:, clipped, head_index]
    return jnp.where(valid[None, :, :, None], picked.astype(jnp.float32), 0.0)


def per_device(queries, keys, values, vert_blocks):
    queries, keys, values = (
        lax.all_to_all(queries, "head", split_axis=1, concat_axis=0, tiled=True),
        lax.all_to_all(keys, "head", split_axis=1, concat_axis=0, tiled=True),
        lax.all_to_all(values, "head", split_axis=1, concat_axis=0, tiled=True),
    )
    rows_here = queries.shape[0]
    groups = vert_blocks.shape[0]
    per_group = H // KVH
    reach = BAND // rows_here
    scale = 1.0 / math.sqrt(DH)
    anchor = lax.axis_index("ctx") * rows_here
    key_value = jnp.stack([keys, values])
    earlier = []
    moving = key_value
    for stride in range(reach):
        moving = shifted(moving, "ctx", 1)
        earlier.insert(0, moving)
    extended = jnp.concatenate(earlier + [key_value], axis=1).reshape(
        2, (reach + 1) * rows_here, groups, DH
    )
    offsets = jnp.arange(VW, dtype=jnp.int32)
    positions = (vert_blocks[:, :, None] * VW + offsets[None, None, :]).reshape(groups, NV)
    own_rows = key_value.reshape(2, rows_here, groups, DH)
    table = lax.psum(select_rows(own_rows, positions, anchor).astype(jnp.bfloat16), "ctx").astype(
        jnp.float32
    )
    table = table.astype(jnp.bfloat16)
    query_block = queries.reshape(QBLK, groups, per_group, DH)
    query_pos = anchor + 0 + jnp.arange(QBLK, dtype=jnp.int32)
    key_pos = anchor + 0 - BAND + jnp.arange(BAND + QBLK, dtype=jnp.int32)
    spacing = query_pos[:, None] - key_pos[None, :]
    band_mask = (spacing >= 0) & (spacing < BAND) & (key_pos[None, :] >= 0)
    band_scores = (
        jnp.einsum("qgpd,kgd->gpqk", query_block, extended[0], preferred_element_type=jnp.float32)
        * scale
    )
    vert_scores = (
        jnp.einsum("qgpd,gkd->gpqk", query_block, table[0], preferred_element_type=jnp.float32)
        * scale
    )
    vert_mask = positions[:, None, None, :] <= (query_pos - BAND)[None, None, :, None]
    band_scores = jnp.where(band_mask[None, None], band_scores, -jnp.inf)
    vert_scores = jnp.where(vert_mask, vert_scores, -jnp.inf)
    top = jnp.maximum(jnp.max(band_scores, axis=-1), jnp.max(vert_scores, axis=-1))
    band_p = jnp.where(band_mask[None, None], jnp.exp(band_scores - top[..., None]), 0.0)
    vert_p = jnp.where(vert_mask, jnp.exp(vert_scores - top[..., None]), 0.0)
    total = jnp.sum(band_p, axis=-1) + jnp.sum(vert_p, axis=-1)
    band_weights = band_p.astype(jnp.bfloat16)
    vert_weights = vert_p.astype(jnp.bfloat16)
    numer = jnp.einsum(
        "gpqk,kgd->qgpd", band_weights, extended[1], preferred_element_type=jnp.float32
    )
    numer = numer + jnp.einsum(
        "gpqk,gkd->qgpd", vert_weights, table[1], preferred_element_type=jnp.float32
    )
    result = numer / jnp.transpose(total, (2, 0, 1))[..., None]
    outputs = result.reshape(QBLK, groups * per_group * DH).astype(jnp.bfloat16)
    return lax.all_to_all(outputs, "head", split_axis=0, concat_axis=1, tiled=True)


def solution(mesh):
    placed = (
        P(("ctx", "head"), None),
        P(("ctx", "head"), None),
        P(("ctx", "head"), None),
        P("head", None),
    )
    return jax.shard_map(
        per_device, mesh=mesh, in_specs=placed, out_specs=P(("ctx", "head"), None), check_vma=False
    )
```

profile of v0, /device:TPU:29, one launch (start us, length us, event | category | flops | bytes accessed | tf_op | source)
XLA Modules:
  0.0 253.2 jit_solution(2018968442913245067)
XLA Ops:
  6.5 0.9 copy-done
  8.1 5.0 %all-to-all-start.1 = ((bf16[64,8,128]{2,0,1:T(8,128)(2,1)}), bf16[64,8,128]{2,0,1:T(8,128)(2,1)S(1)}, u32[]{:S(2)}, u32[]{:S(2)}) async-start(bf16[64,8,128]{2,0,1:T(8,128)(2,1)} %copy_bitcast_fusion.1), calls=%async_computation.1 | async-start | bytes 262144 | tf_op jit(solution)/shard_map/all_to_all | solution.py:37
  13.1 1.6 copy_bitcast_fusion.2
  14.7 2.0 all-to-all-done.1
  16.7 5.9 %all-to-all-start = ((bf16[64,8,128]{2,0,1:T(8,128)(2,1)}), bf16[64,8,128]{2,0,1:T(8,128)(2,1)S(1)}, u32[]{:S(2)}, u32[]{:S(2)}) async-start(bf16[64,8,128]{2,0,1:T(8,128)(2,1)} %copy_bitcast_fusion.2), calls=%async_computation | async-start | bytes 262144 | tf_op jit(solution)/shard_map/all_to_all | solution.py:36
  22.6 2.1 fusion.15
  24.6 2.3 copy.60
  26.9 5.3 %all-to-all-start.2 = ((bf16[64,8,1024]{2,0,1:T(8,128)(2,1)}), bf16[64,8,1024]{2,0,1:T(8,128)(2,1)S(1)}, u32[]{:S(2)}, u32[]{:S(2)}) async-start(bf16[64,8,1024]{2,0,1:T(8,128)(2,1)} %bitcast.132), calls=%async_computation.2 | async-start | bytes 2097152 | tf_op jit(solution)/shard_map/all_to_all | solution.py:35
  32.2 3.5 %collective-permute-start = (bf16[2,512,128]{2,1,0:T(8,128)(2,1)S(1)}, bf16[2,512,128]{2,1,0:T(8,128)(2,1)S(1)}, u32[]{:S(2)}, u32[]{:S(2)}) collective-permute-start(bf16[2,512,128]{2,1,0:T(8,128)(2,1)S(1)} %pad_maximum_fusion), channel_id=1, source_target_pairs={{0,8},{8,16},{16,24},{24,32},{32,40},{40,48},{48,56},{56,64},{64,7... | collective-permute-start | bytes 786440 | tf_op jit(solution)/shard_map/ppermute | solution.py:20
  36.5 7.6 %collective-permute-done = bf16[2,512,128]{2,1,0:T(8,128)(2,1)S(1)} collective-permute-done((bf16[2,512,128]{2,1,0:T(8,128)(2,1)S(1)}, bf16[2,512,128]{2,1,0:T(8,128)(2,1)S(1)}, u32[]{:S(2)}, u32[]{:S(2)}) %collective-permute-start) | collective-permute-done | bytes 262176 | tf_op jit(solution)/shard_map/ppermute | solution.py:20
  44.1 1.9 collective-permute-start.1
  46.1 8.8 %collective-permute-done.1 = bf16[2,512,128]{2,1,0:T(8,128)(2,1)S(1)} collective-permute-done((bf16[2,512,128]{2,1,0:T(8,128)(2,1)S(1)}, bf16[2,512,128]{2,1,0:T(8,128)(2,1)S(1)}, u32[]{:S(2)}, u32[]{:S(2)}) %collective-permute-start.1) | collective-permute-done | bytes 262176 | tf_op jit(solution)/shard_map/ppermute | solution.py:20
  54.9 1.9 collective-permute-start.2
  56.9 8.0 %collective-permute-done.2 = bf16[2,512,128]{2,1,0:T(8,128)(2,1)} collective-permute-done((bf16[2,512,128]{2,1,0:T(8,128)(2,1)S(1)}, bf16[2,512,128]{2,1,0:T(8,128)(2,1)}, u32[]{:S(2)}, u32[]{:S(2)}) %collective-permute-start.2) | collective-permute-done | bytes 262176 | tf_op jit(solution)/shard_map/ppermute | solution.py:20
  64.9 1.9 collective-permute-start.3
  67.2 1.0 copy-done.2
  68.2 1.5 copy.47
  69.7 4.7 %collective-permute-done.3 = bf16[2,512,128]{2,1,0:T(8,128)(2,1)} collective-permute-done((bf16[2,512,128]{2,1,0:T(8,128)(2,1)}, bf16[2,512,128]{2,1,0:T(8,128)(2,1)}, u32[]{:S(2)}, u32[]{:S(2)}) %collective-permute-start.3) | collective-permute-done | bytes 262176 | tf_op jit(solution)/shard_map/ppermute | solution.py:20
  74.4 1.0 constant_dynamic-update-slice_fusion.4
  75.4 1.0 constant_dynamic-update-slice_fusion.3
  76.4 1.0 constant_dynamic-update-slice_fusion.2
  78.5 7.4 %gather_fusion = bf16[1024,2,128]{2,1,0:T(2,128)(2,1)} fusion(bf16[2,512,1,128]{3,0,2,1:T(2,128)(2,1)S(1)} %copy.28, s32[1024]{0:T(1024)S(1)} %bitcast.133), kind=kCustom, calls=%fused_computation | custom fusion | bytes 1056768 | tf_op jit(solution)/shard_map/gather | solution.py:29
  85.9 2.0 fusion.19
  88.0 17.9 %fusion = (f32[8,512]{1,0:T(8,128)S(1)}, f32[2560,512,8]{1,0,2:T(8,128)}) fusion(pred[512,2560]{0,1:T(8,128)(4,1)S(1)} %fusion.15, bf16[512,8,128]{2,1,0:T(8,128)(2,1)S(1)} %bitcast.134, bf16[2,2560,128]{2,1,0:T(8,128)(2,1)} %copy-done.3), kind=kOutput, calls=%fused_computation.3 | convolution fusion | flops 2715807744 | bytes 44974080 | tf_op jit(solution)/shard_map/qgpd,kgd->gpqk/dot_general | solution.py:67
  105.9 66.8 %all-reduce.3.cloned.1.call-done = bf16[2,1,1024,128]{3,2,1,0:T(8,128)(2,1)} async-done(((bf16[2,1,1024,128]{3,2,1,0:T(8,128)(2,1)}), bf16[2,1,1024,128]{3,2,1,0:T(8,128)(2,1)}) %all-reduce.3.cloned.1.call-update) | async-done | bytes 524304 | tf_op jit(solution)/shard_map/psum | solution.py:57
  172.7 3.7 %fusion.7 = (f32[8,512]{1,0:T(8,128)S(1)}, f32[1024,512,8]{1,0,2:T(8,128)S(1)}) fusion(pred[512,1024]{0,1:T(8,128)(4,1)S(1)} %broadcast_compare_fusion, bf16[512,8,128]{2,1,0:T(8,128)(2,1)S(1)} %bitcast.135, bf16[2,1,1024,128]{3,2,1,0:T(8,128)(2,1)} %all-reduce.3.cloned.1.call-done), kind=kOutput, calls=%fused_computation.11 | convolution fusion | flops 1086320640 | bytes 18628608 | tf_op jit(solution)/shard_map/qgpd,gkd->gpqk/dot_general | solution.py:71
  176.4 18.3 %fusion.1 = f32[8,512]{1,0:T(8,128)S(1)} fusion(f32[2560,512,8]{1,0,2:T(8,128)} %get-tuple-element.8, f32[8,512]{1,0:T(8,128)S(1)} %max.13, pred[512,2560]{0,1:T(8,128)(4,1)S(1)} %fusion.15), kind=kLoop, calls=%fused_computation.4 | loop fusion | flops 52424704 | bytes 43286528 | tf_op jit(solution)/shard_map/reduce_sum | solution.py:80
  194.8 4.0 %fusion.8 = f32[8,512]{1,0:T(8,128)S(1)} fusion(f32[1024,512,8]{1,0,2:T(8,128)S(1)} %get-tuple-element.10, f32[8,512]{1,0:T(8,128)S(1)} %max.13, pred[512,1024]{0,1:T(8,128)(4,1)S(1)} %broadcast_compare_fusion), kind=kLoop, calls=%fused_computation.12 | loop fusion | flops 20967424 | bytes 17334272 | tf_op jit(solution)/shard_map/reduce_sum | solution.py:80
  198.8 5.6 %fusion.11 = f32[128,8,512]{2,0,1:T(8,128)} fusion(f32[1024,512,8]{1,0,2:T(8,128)S(1)} %get-tuple-element.10, f32[8,512]{1,0:T(8,128)S(1)} %max.13, pred[512,1024]{0,1:T(8,128)(4,1)S(1)} %broadcast_compare_fusion, bf16[2,1,1024,128]{3,2,1,0:T(8,128)(2,1)S(1)} %copy-done.5), kind=kOutput, calls=%fused_computation.15 | convolution fusion | flops 1094713344 | bytes 19677184 | tf_op jit(solution)/shard_map/gpqk,gkd->qgpd/dot_general | solution.py:86
  204.4 19.3 %fusion.16 = bf16[512,1,8,128]{0,3,2,1:T(8,128)(2,1)S(1)} fusion(f32[128,8,512]{2,0,1:T(8,128)} %fusion.11, f32[2560,512,8]{1,0,2:T(8,128)} %get-tuple-element.8, f32[8,512]{1,0:T(8,128)S(1)} %max.13, pred[512,2560]{0,1:T(8,128)(4,1)S(1)} %fusion.15, f32[512,8]{0,1:T(8,128)S(1)} %add_bitcast_fusion, bf16[2,2560,128]{2,1,0:T(8,128)(2,1)} %copy-done.3), kind=kOutput, calls=%fused_computation.22 | convolution fusion | flops 2738356224 | bytes 47087616 | tf_op jit(solution)/shard_map/gpqk,kgd->qgpd/dot_general | solution.py:83
  225.0 20.4 %all_to_all.64 = bf16[8,64,1024]{2,1,0:T(8,128)(2,1)S(1)} all-to-all(bf16[8,64,1024]{2,1,0:T(8,128)(2,1)S(1)} %convert_element_type.42), channel_id=1, replica_groups=mesh['ctx'=16,'head'=8] {'head'}, dimensions={0} | all-to-all | bytes 2097152 | tf_op jit(solution)/shard_map/all_to_all | solution.py:91
  245.3 1.1 copy.46
  (36 shorter events, 4.4 us)
Async XLA Ops:
  6.5 0.9 copy-start
  8.1 8.6 %all-to-all-start.1 = ((bf16[64,8,128]{2,0,1:T(8,128)(2,1)}), bf16[64,8,128]{2,0,1:T(8,128)(2,1)S(1)}, u32[]{:S(2)}, u32[]{:S(2)}) async-start(bf16[64,8,128]{2,0,1:T(8,128)(2,1)} %copy_bitcast_fusion.1), calls=%async_computation.1 | async-start | bytes 262144 | tf_op jit(solution)/shard_map/all_to_all | solution.py:37
  16.7 10.2 %all-to-all-start = ((bf16[64,8,128]{2,0,1:T(8,128)(2,1)}), bf16[64,8,128]{2,0,1:T(8,128)(2,1)S(1)}, u32[]{:S(2)}, u32[]{:S(2)}) async-start(bf16[64,8,128]{2,0,1:T(8,128)(2,1)} %copy_bitcast_fusion.2), calls=%async_computation | async-start | bytes 262144 | tf_op jit(solution)/shard_map/all_to_all | solution.py:36
  26.9 40.3 %all-to-all-start.2 = ((bf16[64,8,1024]{2,0,1:T(8,128)(2,1)}), bf16[64,8,1024]{2,0,1:T(8,128)(2,1)S(1)}, u32[]{:S(2)}, u32[]{:S(2)}) async-start(bf16[64,8,1024]{2,0,1:T(8,128)(2,1)} %bitcast.132), calls=%async_computation.2 | async-start | bytes 2097152 | tf_op jit(solution)/shard_map/all_to_all | solution.py:35
  32.2 140.5 %all-reduce.3.cloned.1.call-start = ((), (), s32[]{:S(2)}) async-start(), calls=%async_computation.4 | async-start | bytes 1048576 | tf_op jit(solution)/shard_map/psum | solution.py:57
  32.2 11.9 %collective-permute-start = (bf16[2,512,128]{2,1,0:T(8,128)(2,1)S(1)}, bf16[2,512,128]{2,1,0:T(8,128)(2,1)S(1)}, u32[]{:S(2)}, u32[]{:S(2)}) collective-permute-start(bf16[2,512,128]{2,1,0:T(8,128)(2,1)S(1)} %pad_maximum_fusion), channel_id=1, source_target_pairs={{0,8},{8,16},{16,24},{24,32},{32,40},{40,48},{48,56},{56,64},{64,7... | collective-permute-start | bytes 786440 | tf_op jit(solution)/shard_map/ppermute | solution.py:20
  44.1 10.8 %collective-permute-start.1 = (bf16[2,512,128]{2,1,0:T(8,128)(2,1)S(1)}, bf16[2,512,128]{2,1,0:T(8,128)(2,1)S(1)}, u32[]{:S(2)}, u32[]{:S(2)}) collective-permute-start(bf16[2,512,128]{2,1,0:T(8,128)(2,1)S(1)} %collective-permute-done), channel_id=1, source_target_pairs={{0,8},{8,16},{16,24},{24,32},{32,40},{40,48},{48,56},{56,64},{64,7... | collective-permute-start | bytes 786440 | tf_op jit(solution)/shard_map/ppermute | solution.py:20
  54.9 11.9 %copy-start.4 = (bf16[2,512,128]{2,1,0:T(8,128)(2,1)}, bf16[2,512,128]{2,1,0:T(8,128)(2,1)S(1)}, u32[]{:S(2)}) copy-start(bf16[2,512,128]{2,1,0:T(8,128)(2,1)S(1)} %collective-permute-done.1) | copy-start | bytes 786436
  54.9 10.0 %collective-permute-start.2 = (bf16[2,512,128]{2,1,0:T(8,128)(2,1)S(1)}, bf16[2,512,128]{2,1,0:T(8,128)(2,1)}, u32[]{:S(2)}, u32[]{:S(2)}) collective-permute-start(bf16[2,512,128]{2,1,0:T(8,128)(2,1)S(1)} %collective-permute-done.1), channel_id=1, source_target_pairs={{0,8},{8,16},{16,24},{24,32},{32,40},{40,48},{48,56},{56,64},{64,7... | collective-permute-start | bytes 786440 | tf_op jit(solution)/shard_map/ppermute | solution.py:20
  64.9 9.5 %collective-permute-start.3 = (bf16[2,512,128]{2,1,0:T(8,128)(2,1)}, bf16[2,512,128]{2,1,0:T(8,128)(2,1)}, u32[]{:S(2)}, u32[]{:S(2)}) collective-permute-start(bf16[2,512,128]{2,1,0:T(8,128)(2,1)} %collective-permute-done.2), channel_id=1, source_target_pairs={{0,8},{8,16},{16,24},{24,32},{32,40},{40,48},{48,56},{56,64},{64,7... | collective-permute-start | bytes 786440 | tf_op jit(solution)/shard_map/ppermute | solution.py:20
  67.2 1.0 copy-start.2
  77.5 1.0 copy-start.3
  194.8 4.1 %copy-start.5 = (bf16[2,1,1024,128]{3,2,1,0:T(8,128)(2,1)S(1)}, bf16[2,1,1024,128]{3,2,1,0:T(8,128)(2,1)}, u32[]{:S(2)}) copy-start(bf16[2,1,1024,128]{3,2,1,0:T(8,128)(2,1)} %all-reduce.3.cloned.1.call-done) | copy-start | bytes 1572868
  204.4 42.0 %copy-start.1 = (bf16[64,1024]{1,0:T(8,128)(2,1)S(1)}, bf16[64,1024]{1,0:T(8,128)(2,1)}, u32[]{:S(2)}) copy-start(bf16[64,1024]{1,0:T(8,128)(2,1)} %param.6) | copy-start | bytes 393220
Sparse Core Ops, SparseCore 0:
  88.1 84.5 all-reduce.2
where the time goes:
time: 258 us; the launch traced here: 253 us
  waiting for transfers between devices  97.9 us (38%)
  matrix products  46.5 us (18%)
  other arithmetic  27.8 us (11%)
  starting transfers between devices  25.4 us (10%)
  local copies, waits for them, and re-layouts  21.7 us (8%)
  blocking collectives  20.4 us (8%)
  between operations  13.7 us (5%)
    psum x1, waiting for transfers between devices, per_device(): lax.psum(select_rows(own_rows, positions, anchor).astype(jnp.bfloat16), '...  66.8 us
    ppermute x4, waiting for transfers between devices, shifted(): return lax.ppermute(shard, axis, pairs)  29.1 us
    reduce_sum x2, other arithmetic, per_device(): total = jnp.sum(band_p, axis=-1) + jnp.sum(vert_p, axis=-1)  22.4 us
    all_to_all x1, blocking collectives, per_device(): lax.all_to_all(outputs, 'head', split_axis=0, concat_axis=1, tiled=True)  20.4 us
    dot_general x1, matrix products, per_device(): jnp.einsum('gpqk,kgd->qgpd', band_weights, extended[1], preferred_element...  19.3 us
    dot_general x1, matrix products, per_device(): jnp.einsum('qgpd,kgd->gpqk', query_block, extended[0], preferred_element_...  17.9 us
    ppermute x4, starting transfers between devices, shifted(): return lax.ppermute(shard, axis, pairs)  9.27 us
    gather x1, local copies, waits for them, and re-layouts, select_rows(): picked = source[:, clipped, head_index]  7.36 us
  transfers between devices with their start and end apart: 8, of which 6 were waited for; matrix products, arithmetic and copies ran while one was open for 11% of the time, Pallas kernels for 0%

commit v1 on v0

v1 whole, which is shorter than its diff:
```python
import functools
import math

import jax
import jax.numpy as jnp
from jax import lax
from jax.experimental import pallas as pl
from jax.experimental.pallas import tpu as pltpu
from jax.sharding import PartitionSpec as P

DH = 128
VW = 128
NVB = 8
NC = 16
NH = 8
ROWS = 64
SLAB = 512
BAND = 2048
HPG = 8
WIDTH = HPG * DH
M = ROWS * HPG
BANDK = BAND + 2 * ROWS
KVROWS = BAND + SLAB + ROWS
NK = BANDK + NVB * VW
KB = 256
NEG = -1e30
SCALE = math.log2(math.e) / math.sqrt(float(DH))

BLOCKS = []
_o = 0
while _o < BANDK:
    _w = min(KB, BANDK - _o)
    BLOCKS.append((0, _o, _w, _o))
    _o += _w
for _b in range(0, NVB * VW, KB):
    BLOCKS.append((1, _b, KB, BANDK + _b))


def kernel(
    q_hbm, k_hbm, v_hbm, vb_ref, out_hbm,
    qb, kv, vt, tb, rb, ch, ob, s_ref, m_ref,
    loc, kvs, kvr, qs, qr, bs, br, rs, rr, gs, gr, os_, or_,
):
    c = lax.axis_index("ctx")
    h = lax.axis_index("head")
    x = c // 4
    z = c % 4
    y = h // 2
    core = h % 2

    def remote(src, dst, ssem, rsem, cc, hh):
        return pltpu.make_async_remote_copy(
            src_ref=src, dst_ref=dst, send_sem=ssem, recv_sem=rsem,
            device_id={"ctx": cc, "head": hh}, device_id_type=pl.DeviceIdType.MESH,
        )

    def drain(ref, sem):
        pltpu.make_async_copy(ref, ref, sem).wait()

    def offset(i):
        j = (i - 1) // 2
        dy = jnp.where(i == 0, 0, jnp.where(i == 7, 0, 1 + 2 * j - 3 * (j // 2)))
        dc = jnp.where(i == 0, 1, jnp.where(i == 7, 0, (i - 1) % 2))
        return dy, dc

    def source(i):
        dy, dc = offset(i)
        return ((y + dy) % 4) * 2 + (core + dc) % 2

    def target(i):
        dy, dc = offset(i)
        return ((y + 4 - dy) % 4) * 2 + (core + 2 - dc) % 2

    def pick(shape, b):
        return jnp.zeros(shape, jnp.int32) + vb_ref[0, b]

    def choose(cases):
        r = jnp.zeros(cases[0][1].shape, jnp.float32)
        for mask, value in cases:
            r = jnp.where(mask, value.astype(jnp.float32), r)
        return r.astype(jnp.bfloat16)

    mine = pl.ds(pl.multiple_of(BAND + h * ROWS, ROWS), ROWS)
    own_k = pltpu.make_async_copy(
        k_hbm.at[:, pl.ds(pl.multiple_of(h * DH, DH), DH)], kv.at[mine, pl.ds(0, DH)], loc.at[0])
    own_v = pltpu.make_async_copy(
        v_hbm.at[:, pl.ds(pl.multiple_of(h * DH, DH), DH)], kv.at[mine, pl.ds(DH, DH)], loc.at[1])
    own_q = pltpu.make_async_copy(
        q_hbm.at[:, pl.ds(pl.multiple_of(h * WIDTH, WIDTH), WIDTH)], qb.at[h], loc.at[2])
    own_k.start()
    own_v.start()
    own_q.start()

    barrier = pltpu.get_barrier_semaphore()
    for d in range(1, NH):
        pl.semaphore_signal(barrier, inc=1, device_id={"ctx": c, "head": (h + d) % NH},
                            device_id_type=pl.DeviceIdType.MESH)
    for d in range(1, NC):
        pl.semaphore_signal(barrier, inc=1, device_id={"ctx": (c + d) % NC, "head": h},
                            device_id_type=pl.DeviceIdType.MESH)
    kv[pl.ds(BAND + SLAB, ROWS), :] = jnp.zeros((ROWS, 2 * DH), jnp.bfloat16)

    @pl.when(c < 4)
    def _():
        vt[...] = jnp.zeros_like(vt)
        for d in range(1, 5):
            @pl.when(c < d)
            def _():
                kv[pl.ds((4 - d) * SLAB, SLAB), :] = jnp.zeros((SLAB, 2 * DH), jnp.bfloat16)

    pl.semaphore_wait(barrier, NH - 1 + NC - 1)

    def kv_copies(i):
        t = target(i)
        return [
            remote(src.at[:, pl.ds(pl.multiple_of(t * DH, DH), DH)],
                   kv.at[mine, pl.ds(n * DH, DH)], kvs.at[t], kvr.at[h], c, t)
            for n, src in enumerate((k_hbm, v_hbm))
        ]

    def q_copy(i):
        t = target(i)
        return remote(q_hbm.at[:, pl.ds(pl.multiple_of(t * WIDTH, WIDTH), WIDTH)],
                      qb.at[h], qs.at[t], qr.at[h], c, t)

    for i in range(7):
        for cp in kv_copies(i):
            cp.start()
    for i in range(7):
        q_copy(i).start()

    own_k.wait()
    own_v.wait()
    for i in range(7):
        s = source(i)
        drain(kv.at[pl.ds(pl.multiple_of(BAND + s * ROWS, ROWS), ROWS), :], kvr.at[s])

    def slab(d):
        return kv.at[pl.ds((4 - d) * SLAB, SLAB), :]

    def hop(n, cond, d_src, d_dst, cc):
        @pl.when(cond)
        def _():
            remote(slab(d_src), slab(d_dst), bs.at[n], br.at[d_dst - 1], cc, h).start()

    def landed(d):
        @pl.when(c >= d)
        def _():
            drain(slab(d), br.at[d - 1])

    row = x * 4

    @pl.when(x < 3)
    def _():
        for b in range(NVB):
            place = pick((VW, 2 * DH), b) - 4 * c
            tb[pl.ds(b * VW, VW), :] = choose(
                [(place == n, kv[pl.ds(BAND + n * VW, VW), :]) for n in range(4)])
        own = pltpu.make_async_copy(tb.at[pl.ds(pl.multiple_of(c * ROWS, ROWS), ROWS), :],
                                    rb.at[c], loc.at[3])
        own.start()
        for d in range(1, NC):
            j = (c + d) % NC
            remote(tb.at[pl.ds(pl.multiple_of(j * ROWS, ROWS), ROWS), :], rb.at[c],
                   rs.at[j], rr.at[c], j, h).start()
        own.wait()

    hop(0, z < 3, 0, 1, c + 1)
    hop(1, z == 0, 0, 3, c + 3)
    hop(2, x < 3, 0, 4, c + 4)

    for s in range(12):
        @pl.when(c != s)
        def _():
            drain(rb.at[s], rr.at[s])
    holder = pick((ROWS, 2 * DH), c // 2)
    ch[...] = choose(
        [((holder >= 4 * s) & (holder < 4 * s + 4), rb[s]) for s in range(12)])
    for d in range(1, NC):
        j = (c + d) % NC

        @pl.when(j >= 4)
        def _():
            remote(ch, vt.at[pl.ds(pl.multiple_of(c * ROWS, ROWS), ROWS), :],
                   gs.at[j], gr.at[c], j, h).start()

    landed(4)
    hop(3, (x > 0) & (z > 0), 4, 3, c - 1)
    hop(4, (x > 0) & (z == 3), 4, 1, c - 3)
    landed(1)
    hop(5, (z == 1) | (z == 2), 1, 2, c + 1)
    landed(3)
    hop(6, (x > 0) & ((z == 1) | (z == 2)), 3, 2, c - 1)
    landed(2)

    @pl.when(c >= 4)
    def _():
        own = pltpu.make_async_copy(ch, vt.at[pl.ds(pl.multiple_of(c * ROWS, ROWS), ROWS), :],
                                    loc.at[4])
        own.start()
        own.wait()
        for s in range(NC):
            @pl.when(c != s)
            def _():
                drain(vt.at[pl.ds(s * ROWS, ROWS), :], gr.at[s])

    ii = lax.broadcasted_iota(jnp.int32, (ROWS, VW), 0)
    jj = lax.broadcasted_iota(jnp.int32, (ROWS, VW), 1)
    missing = jnp.maximum(BAND - c * SLAB, 0)

    def keep(mask, t):
        return jnp.where(mask[None], t.reshape(HPG, ROWS, VW), NEG).reshape(M, VW)

    def load_q(p):
        return jnp.concatenate([qb[p, :, n * DH:(n + 1) * DH] for n in range(HPG)], axis=0)

    def scores(p, q, blk, slot, mx):
        kind, off, w, col = blk
        base = pl.multiple_of(p * ROWS, ROWS)
        k = kv[pl.ds(base + off, w), :DH] if kind == 0 else vt[off:off + w, :DH]
        s = lax.dot_general(q, k, (((1,), (1,)), ((), ())), preferred_element_type=jnp.float32)
        for t in range(w // VW):
            e = s[:, t * VW:(t + 1) * VW]
            o = off + t * VW
            if kind == 0:
                mask = jj >= missing - base - o
                if o == 0:
                    mask = mask & (jj > ii)
                if o + VW == BANDK:
                    mask = mask & (jj <= ii)
            else:
                mask = (jj - ii + pick((ROWS, VW), o // VW) * VW) <= (c * SLAB + p * ROWS - BAND)
            e = keep(mask, e)
            mx = e if mx is None else jnp.maximum(mx, e)
            s_ref[slot, :, col + t * VW:col + (t + 1) * VW] = e
        return mx

    def finish_max(mx, slot):
        m_ref[slot] = jnp.broadcast_to(jnp.max(mx, axis=1, keepdims=True) * SCALE, (M, VW))

    def weigh(p, blk, slot, acc):
        kind, off, w, col = blk
        base = pl.multiple_of(p * ROWS, ROWS)
        v = kv[pl.ds(base + off, w), DH:] if kind == 0 else vt[off:off + w, DH:]
        v = jnp.concatenate([v, jnp.ones((w, DH), jnp.bfloat16)], axis=1)
        m = m_ref[slot]
        e = [jnp.exp2(s_ref[slot, :, col + t * VW:col + (t + 1) * VW] * SCALE - m).astype(jnp.bfloat16)
             for t in range(w // VW)]
        d = jnp.dot(jnp.concatenate(e, axis=1), v, preferred_element_type=jnp.float32)
        return d if acc is None else acc + d

    def out_copy(p):
        return remote(ob.at[p], out_hbm.at[:, pl.ds(pl.multiple_of(h * WIDTH, WIDTH), WIDTH)],
                      os_.at[p], or_.at[h], c, p)

    def stage(i, slot):
        p = source(i)
        n = source(jnp.minimum(i + 1, 7))

        @pl.when(i < 6)
        def _():
            drain(qb.at[n], qr.at[n])

        q = load_q(n)
        acc = mx = None
        for blk in BLOCKS:
            mx = scores(n, q, blk, 1 - slot, mx)
            acc = weigh(p, blk, slot, acc)
        finish_max(mx, 1 - slot)
        o = (acc[:, :DH] / acc[:, DH:]).astype(jnp.bfloat16)
        for t in range(HPG):
            ob[p, :, t * DH:(t + 1) * DH] = o[t * ROWS:(t + 1) * ROWS]

        @pl.when(i < 7)
        def _():
            out_copy(p).start()

    own_q.wait()
    first = source(0)
    drain(qb.at[first], qr.at[first])
    q = load_q(first)
    mx = None
    for blk in BLOCKS:
        mx = scores(first, q, blk, 0, mx)
    finish_max(mx, 0)

    def body(t, carry):
        stage(2 * t, 0)
        stage(2 * t + 1, 1)
        return carry

    lax.fori_loop(0, 4, body, 0)

    own_o = pltpu.make_async_copy(
        ob.at[h], out_hbm.at[:, pl.ds(pl.multiple_of(h * WIDTH, WIDTH), WIDTH)], loc.at[5])
    own_o.start()

    for i in range(7):
        t = target(i)
        for cp in kv_copies(i):
            cp.wait_send()
        q_copy(i).wait_send()
    for n, cond, d in (
        (0, z < 3, 0), (1, z == 0, 0), (2, x < 3, 0), (3, (x > 0) & (z > 0), 4),
        (4, (x > 0) & (z == 3), 4), (5, (z == 1) | (z == 2), 1),
        (6, (x > 0) & ((z == 1) | (z == 2)), 3),
    ):
        @pl.when(cond)
        def _():
            drain(slab(d), bs.at[n])
    for d in range(1, NC):
        j = (c + d) % NC

        @pl.when(x < 3)
        def _():
            drain(rb.at[0], rs.at[j])

        @pl.when(j >= 4)
        def _():
            drain(ch, gs.at[j])
    for i in range(7):
        p = source(i)
        drain(ob.at[p], os_.at[p])
        drain(out_hbm.at[:, pl.ds(pl.multiple_of(p * WIDTH, WIDTH), WIDTH)], or_.at[p])
    own_o.wait()


def per_device(queries, keys, values, vert_blocks):
    anywhere = pl.BlockSpec(memory_space=pl.ANY)
    dma = pltpu.SemaphoreType.DMA
    bf = jnp.bfloat16
    return pl.pallas_call(
        kernel,
        out_shape=jax.ShapeDtypeStruct((ROWS, NH * WIDTH), bf),
        in_specs=[anywhere, anywhere, anywhere, pl.BlockSpec(memory_space=pltpu.SMEM)],
        out_specs=anywhere,
        scratch_shapes=[
            pltpu.VMEM((NH, ROWS, WIDTH), bf),
            pltpu.VMEM((KVROWS, 2 * DH), bf),
            pltpu.VMEM((NVB * VW, 2 * DH), bf),
            pltpu.VMEM((NVB * VW, 2 * DH), bf),
            pltpu.VMEM((12, ROWS, 2 * DH), bf),
            pltpu.VMEM((ROWS, 2 * DH), bf),
            pltpu.VMEM((NH, ROWS, WIDTH), bf),
            pltpu.VMEM((2, M, NK), jnp.float32),
            pltpu.VMEM((2, M, VW), jnp.float32),
            dma((8,)), dma((NH,)), dma((NH,)), dma((NH,)), dma((NH,)),
            dma((8,)), dma((4,)), dma((NC,)), dma((12,)), dma((NC,)), dma((NC,)),
            dma((NH,)), dma((NH,)),
        ],
        compiler_params=pltpu.CompilerParams(
            collective_id=0, has_side_effects=True, vmem_limit_bytes=60 * 2**20),
        name="sparse_attention",
    )(queries, keys, values, vert_blocks)


def solution(mesh):
    placed = (
        P(("ctx", "head"), None),
        P(("ctx", "head"), None),
        P(("ctx", "head"), None),
        P("head", None),
    )
    return jax.shard_map(
        per_device, mesh=mesh, in_specs=placed, out_specs=P(("ctx", "head"), None), check_vma=False
    )
```

time: 258 us -> 70.9 us (0.27); the launches traced: 253 us -> 70.8 us
  waiting for transfers between devices: 97.9 us -> 0 us
  Pallas kernels: 0 us -> 68.5 us
  matrix products: 46.5 us -> 0 us
  other arithmetic: 27.8 us -> 0 us
  starting transfers between devices: 25.4 us -> 0 us
  blocking collectives: 20.4 us -> 0 us
  local copies, waits for them, and re-layouts: 21.7 us -> 2.26 us
  between operations: 13.7 us -> 0.01 us
    pallas_call x0 -> x1, Pallas kernels: none -> 68.5 us  [per_device(): pl.pallas_call(kernel, out_shape=jax.ShapeDtypeStruct((ROWS, NH * WIDTH),...]
    psum x1 -> x0, waiting for transfers between devices: 66.8 us -> none  [per_device(): lax.psum(select_rows(own_rows, positions, anchor).astype(jnp.bfloat16), '...]
    dot_general x4 -> x0, matrix products: 46.5 us -> none  [the longest x1 19.3 us: per_device(): jnp.einsum('gpqk,kgd->qgpd', band_weights, extended[1], preferred_element...]
    ppermute x4 -> x0, waiting for transfers between devices: 29.1 us -> none  [shifted(): return lax.ppermute(shard, axis, pairs)]
    reduce_sum x2 -> x0, other arithmetic: 22.4 us -> none  [per_device(): total = jnp.sum(band_p, axis=-1) + jnp.sum(vert_p, axis=-1)]
    all_to_all x1 -> x0, blocking collectives: 20.4 us -> none  [per_device(): lax.all_to_all(outputs, 'head', split_axis=0, concat_axis=1, tiled=True)]
    all_to_all x3 -> x0, starting transfers between devices: 16.1 us -> none  [the longest x1 5.88 us: per_device(): lax.all_to_all(keys, 'head', split_axis=1, concat_axis=0, tiled=True)]
    ppermute x4 -> x0, starting transfers between devices: 9.27 us -> none  [shifted(): return lax.ppermute(shard, axis, pairs)]
  transfers between devices with their start and end apart: 8 -> 0, of which waited for: 6 -> 0; matrix products, arithmetic and copies ran while one was open for 11% -> 0% of each run, Pallas kernels for 0% -> 0%
where the time goes in v1:
time: 70.9 us; the launch traced here: 70.8 us
  Pallas kernels  68.5 us (97%)
  local copies, waits for them, and re-layouts  2.26 us (3%)
    pallas_call x1, Pallas kernels, per_device(): pl.pallas_call(kernel, out_shape=jax.ShapeDtypeStruct((ROWS, NH * WIDTH),...  68.5 us
    unnamed x1, local copies, waits for them, and re-layouts  2.26 us

profile of v1, /device:TPU:29, one launch (start us, length us, event | category | flops | bytes accessed | tf_op | source)
XLA Modules:
  0.0 70.8 jit_solution(15342550435330902667)
XLA Ops:
  0.0 68.5 %sparse_attention.1 = bf16[64,8192]{1,0:T(8,128)(2,1)} custom-call(bf16[64,8192]{1,0:T(8,128)(2,1)} %q_hbm.1, bf16[64,1024]{1,0:T(8,128)(2,1)} %k_hbm.1, bf16[64,1024]{1,0:T(8,128)(2,1)} %v_hbm.1, s32[1,8]{1,0:T(1,128)} %vb_ref.1), custom_call_target="tpu_custom_call" | custom-call | tf_op jit(solution)/shard_map/sparse_attention/pallas_call | solution.py:332
  68.5 2.3 %copy.6 = bf16[64,8192]{1,0:T(8,128)(2,1)} copy(bf16[64,8192]{1,0:T(8,128)(2,1)} %sparse_attention.1) | data formatting | bytes 2097152

commit v2 on v1

--- a/solution.py
+++ b/solution.py
@@ -23,6 +23,8 @@
 KVROWS = BAND + SLAB + ROWS
 NK = BANDK + NVB * VW
 KB = 256
+PIECE = 128
+NPIECE = SLAB // PIECE
 NEG = -1e30
 SCALE = math.log2(math.e) / math.sqrt(float(DH))
 
@@ -38,7 +40,7 @@
 
 def kernel(
     q_hbm, k_hbm, v_hbm, vb_ref, out_hbm,
-    qb, kv, vt, tb, rb, ch, ob, s_ref, m_ref,
+    qb, kv, vt, tb, rb, ch, ob, s_ref, m_ref, va, vm,
     loc, kvs, kvr, qs, qr, bs, br, rs, rr, gs, gr, os_, or_,
 ):
     c = lax.axis_index("ctx")
@@ -138,71 +140,83 @@
     def slab(d):
         return kv.at[pl.ds((4 - d) * SLAB, SLAB), :]
 
-    def hop(n, cond, d_src, d_dst, cc):
+    def piece(d, k):
+        return kv.at[pl.ds((4 - d) * SLAB + k * PIECE, PIECE), :]
+
+    def hop(n, cond, d_src, d_dst, cc, k):
         @pl.when(cond)
         def _():
-            remote(slab(d_src), slab(d_dst), bs.at[n], br.at[d_dst - 1], cc, h).start()
-
-    def landed(d):
+            remote(piece(d_src, k), piece(d_dst, k), bs.at[n], br.at[d_dst - 1, k], cc, h).start()
+
+    def landed(d, k):
         @pl.when(c >= d)
         def _():
-            drain(slab(d), br.at[d - 1])
-
-    row = x * 4
-
-    @pl.when(x < 3)
-    def _():
-        for b in range(NVB):
-            place = pick((VW, 2 * DH), b) - 4 * c
-            tb[pl.ds(b * VW, VW), :] = choose(
-                [(place == n, kv[pl.ds(BAND + n * VW, VW), :]) for n in range(4)])
-        own = pltpu.make_async_copy(tb.at[pl.ds(pl.multiple_of(c * ROWS, ROWS), ROWS), :],
-                                    rb.at[c], loc.at[3])
-        own.start()
+            drain(piece(d, k), br.at[d - 1, k])
+
+    middle = (z == 1) | (z == 2)
+    back = x > 0
+
+    def table_send():
+        @pl.when(x < 3)
+        def _():
+            for b in range(NVB):
+                place = pick((VW, 2 * DH), b) - 4 * c
+                tb[pl.ds(b * VW, VW), :] = choose(
+                    [(place == n, kv[pl.ds(BAND + n * VW, VW), :]) for n in range(4)])
+            own = pltpu.make_async_copy(tb.at[pl.ds(pl.multiple_of(c * ROWS, ROWS), ROWS), :],
+                                        rb.at[c], loc.at[3])
+            own.start()
+            for d in range(1, NC):
+                j = (c + d) % NC
+                remote(tb.at[pl.ds(pl.multiple_of(j * ROWS, ROWS), ROWS), :], rb.at[c],
+                       rs.at[j], rr.at[c], j, h).start()
+            own.wait()
+
+    def table_spread():
+        for s in range(12):
+            @pl.when(c != s)
+            def _():
+                drain(rb.at[s], rr.at[s])
+        holder = pick((ROWS, 2 * DH), c // 2)
+        ch[...] = choose(
+            [((holder >= 4 * s) & (holder < 4 * s + 4), rb[s]) for s in range(12)])
         for d in range(1, NC):
             j = (c + d) % NC
-            remote(tb.at[pl.ds(pl.multiple_of(j * ROWS, ROWS), ROWS), :], rb.at[c],
-                   rs.at[j], rr.at[c], j, h).start()
-        own.wait()
-
-    hop(0, z < 3, 0, 1, c + 1)
-    hop(1, z == 0, 0, 3, c + 3)
-    hop(2, x < 3, 0, 4, c + 4)
-
-    for s in range(12):
-        @pl.when(c != s)
-        def _():
-            drain(rb.at[s], rr.at[s])
-    holder = pick((ROWS, 2 * DH), c // 2)
-    ch[...] = choose(
-        [((holder >= 4 * s) & (holder < 4 * s + 4), rb[s]) for s in range(12)])
-    for d in range(1, NC):
-        j = (c + d) % NC
-
-        @pl.when(j >= 4)
-        def _():
-            remote(ch, vt.at[pl.ds(pl.multiple_of(c * ROWS, ROWS), ROWS), :],
-                   gs.at[j], gr.at[c], j, h).start()
-
-    landed(4)
-    hop(3, (x > 0) & (z > 0), 4, 3, c - 1)
-    hop(4, (x > 0) & (z == 3), 4, 1, c - 3)
-    landed(1)
-    hop(5, (z == 1) | (z == 2), 1, 2, c + 1)
-    landed(3)
-    hop(6, (x > 0) & ((z == 1) | (z == 2)), 3, 2, c - 1)
-    landed(2)
-
-    @pl.when(c >= 4)
-    def _():
-        own = pltpu.make_async_copy(ch, vt.at[pl.ds(pl.multiple_of(c * ROWS, ROWS), ROWS), :],
-                                    loc.at[4])
-        own.start()
-        own.wait()
-        for s in range(NC):
-            @pl.when(c != s)
+
+            @pl.when(j >= 4)
             def _():
-                drain(vt.at[pl.ds(s * ROWS, ROWS), :], gr.at[s])
+                remote(ch, vt.at[pl.ds(pl.multiple_of(c * ROWS, ROWS), ROWS), :],
+                       gs.at[j], gr.at[c], j, h).start()
+
+    def table_wait():
+        @pl.when(c >= 4)
+        def _():
+            own = pltpu.make_async_copy(ch, vt.at[pl.ds(pl.multiple_of(c * ROWS, ROWS), ROWS), :],
+                                        loc.at[4])
+            own.start()
+            own.wait()
+            for s in range(NC):
+                @pl.when(c != s)
+                def _():
+                    drain(vt.at[pl.ds(s * ROWS, ROWS), :], gr.at[s])
+
+    table_send()
+    for k in range(NPIECE):
+        hop(2, x < 3, 0, 4, c + 4, k)
+        hop(0, z < 3, 0, 1, c + 1, k)
+        hop(1, z == 0, 0, 3, c + 3, k)
+    table_spread()
+    for k in range(NPIECE):
+        landed(4, k)
+        hop(3, back & (z > 0), 4, 3, c - 1, k)
+        hop(4, back & (z == 3), 4, 1, c - 3, k)
+    for k in range(NPIECE):
+        landed(1, k)
+        hop(5, middle, 1, 2, c + 1, k)
+    for k in range(NPIECE):
+        landed(3, k)
+        hop(6, back & middle, 3, 2, c - 1, k)
+    table_wait()
 
     ii = lax.broadcasted_iota(jnp.int32, (ROWS, VW), 0)
     jj = lax.broadcasted_iota(jnp.int32, (ROWS, VW), 1)
@@ -235,8 +249,8 @@
             s_ref[slot, :, col + t * VW:col + (t + 1) * VW] = e
         return mx
 
-    def finish_max(mx, slot):
-        m_ref[slot] = jnp.broadcast_to(jnp.max(mx, axis=1, keepdims=True) * SCALE, (M, VW))
+    def row_max(mx):
+        return jnp.broadcast_to(jnp.max(mx, axis=1, keepdims=True) * SCALE, (M, VW))
 
     def weigh(p, blk, slot, acc):
         kind, off, w, col = blk
@@ -253,20 +267,66 @@
         return remote(ob.at[p], out_hbm.at[:, pl.ds(pl.multiple_of(h * WIDTH, WIDTH), WIDTH)],
                       os_.at[p], or_.at[h], c, p)
 
-    def stage(i, slot):
-        p = source(i)
-        n = source(jnp.minimum(i + 1, 7))
-
-        @pl.when(i < 6)
-        def _():
+    def unit_loop(blocks, before, top, after):
+        def begin(i):
+            before(i)
+            return source(i)
+
+        def stage(i, slot):
+            p = source(i)
+            n = begin(jnp.minimum(i + 1, 7))
+            q = load_q(n)
+            acc = mx = None
+            for blk in blocks:
+                mx = scores(n, q, blk, 1 - slot, mx)
+                acc = weigh(p, blk, slot, acc)
+            after(i, p, slot, acc)
+            m_ref[1 - slot] = top(n, row_max(mx))
+
+        n = begin(0)
+        q = load_q(n)
+        mx = None
+        for blk in blocks:
+            mx = scores(n, q, blk, 0, mx)
+        m_ref[0] = top(n, row_max(mx))
+
+        def body(t, carry):
+            stage(2 * t, 0)
+            stage(2 * t + 1, 1)
+            return carry
+
+        lax.fori_loop(0, 4, body, 0)
+
+    own_q.wait()
+
+    def q_arrived(i):
+        @pl.when(i < 7)
+        def _():
+            n = source(i)
             drain(qb.at[n], qr.at[n])
 
-        q = load_q(n)
-        acc = mx = None
-        for blk in BLOCKS:
-            mx = scores(n, q, blk, 1 - slot, mx)
-            acc = weigh(p, blk, slot, acc)
-        finish_max(mx, 1 - slot)
+    def keep_vertical(i, p, slot, acc):
+        va[p] = acc
+        vm[p] = m_ref[slot]
+
+    @pl.when(c >= 4)
+    def _():
+        unit_loop([blk for blk in BLOCKS if blk[0] == 1],
+                  lambda i: q_arrived(i), lambda n, m: m, keep_vertical)
+
+    @pl.when(c < 4)
+    def _():
+        va[...] = jnp.zeros_like(va)
+        vm[...] = jnp.full_like(vm, NEG)
+        for i in range(7):
+            q_arrived(i)
+
+    for k in range(NPIECE):
+        landed(2, k)
+
+    def finish(i, p, slot, acc):
+        f = jnp.exp2(vm[p] - m_ref[slot])
+        acc = acc + va[p] * jnp.concatenate([f, f], axis=1)
         o = (acc[:, :DH] / acc[:, DH:]).astype(jnp.bfloat16)
         for t in range(HPG):
             ob[p, :, t * DH:(t + 1) * DH] = o[t * ROWS:(t + 1) * ROWS]
@@ -275,21 +335,8 @@
         def _():
             out_copy(p).start()
 
-    own_q.wait()
-    first = source(0)
-    drain(qb.at[first], qr.at[first])
-    q = load_q(first)
-    mx = None
-    for blk in BLOCKS:
-        mx = scores(first, q, blk, 0, mx)
-    finish_max(mx, 0)
-
-    def body(t, carry):
-        stage(2 * t, 0)
-        stage(2 * t + 1, 1)
-        return carry
-
-    lax.fori_loop(0, 4, body, 0)
+    unit_loop([blk for blk in BLOCKS if blk[0] == 0],
+              lambda i: None, lambda n, m: jnp.maximum(m, vm[n]), finish)
 
     own_o = pltpu.make_async_copy(
         ob.at[h], out_hbm.at[:, pl.ds(pl.multiple_of(h * WIDTH, WIDTH), WIDTH)], loc.at[5])
@@ -301,9 +348,8 @@
             cp.wait_send()
         q_copy(i).wait_send()
     for n, cond, d in (
-        (0, z < 3, 0), (1, z == 0, 0), (2, x < 3, 0), (3, (x > 0) & (z > 0), 4),
-        (4, (x > 0) & (z == 3), 4), (5, (z == 1) | (z == 2), 1),
-        (6, (x > 0) & ((z == 1) | (z == 2)), 3),
+        (0, z < 3, 0), (1, z == 0, 0), (2, x < 3, 0), (3, back & (z > 0), 4),
+        (4, back & (z == 3), 4), (5, middle, 1), (6, back & middle, 3),
     ):
         @pl.when(cond)
         def _():
@@ -344,8 +390,10 @@
             pltpu.VMEM((NH, ROWS, WIDTH), bf),
             pltpu.VMEM((2, M, NK), jnp.float32),
             pltpu.VMEM((2, M, VW), jnp.float32),
+            pltpu.VMEM((NH, M, 2 * DH), jnp.float32),
+            pltpu.VMEM((NH, M, VW), jnp.float32),
             dma((8,)), dma((NH,)), dma((NH,)), dma((NH,)), dma((NH,)),
-            dma((8,)), dma((4,)), dma((NC,)), dma((12,)), dma((NC,)), dma((NC,)),
+            dma((8,)), dma((4, NPIECE)), dma((NC,)), dma((12,)), dma((NC,)), dma((NC,)),
             dma((NH,)), dma((NH,)),
         ],
         compiler_params=pltpu.CompilerParams(

time: 70.9 us -> 68.2 us (0.962)
  Pallas kernels: 68.5 us -> 65.8 us
    pallas_call x1, Pallas kernels: 68.5 us -> 65.8 us  [per_device(): pl.pallas_call(kernel, out_shape=jax.ShapeDtypeStruct((ROWS, NH * WIDTH),...]
where the time goes in v2:
time: 68.2 us; the launch traced here: 68 us
  Pallas kernels  65.8 us (96%)
  local copies, waits for them, and re-layouts  2.26 us (3%)
    pallas_call x1, Pallas kernels, per_device(): pl.pallas_call(kernel, out_shape=jax.ShapeDtypeStruct((ROWS, NH * WIDTH),...  65.8 us
    unnamed x1, local copies, waits for them, and re-layouts  2.26 us

profile of v2, /device:TPU:29, one launch (start us, length us, event | category | flops | bytes accessed | tf_op | source)
XLA Modules:
  0.0 68.0 jit_solution(5881040256080347904)
XLA Ops:
  0.0 65.8 %sparse_attention.1 = bf16[64,8192]{1,0:T(8,128)(2,1)} custom-call(bf16[64,8192]{1,0:T(8,128)(2,1)} %q_hbm.1, bf16[64,1024]{1,0:T(8,128)(2,1)} %k_hbm.1, bf16[64,1024]{1,0:T(8,128)(2,1)} %v_hbm.1, s32[1,8]{1,0:T(1,128)} %vb_ref.1), custom_call_target="tpu_custom_call" | custom-call | tf_op jit(solution)/shard_map/sparse_attention/pallas_call | solution.py:378
  65.8 2.3 %copy.6 = bf16[64,8192]{1,0:T(8,128)(2,1)} copy(bf16[64,8192]{1,0:T(8,128)(2,1)} %sparse_attention.1) | data formatting | bytes 2097152

commit v3 on v2

--- a/solution.py
+++ b/solution.py
@@ -40,8 +40,9 @@
 
 def kernel(
     q_hbm, k_hbm, v_hbm, vb_ref, out_hbm,
-    qb, kv, vt, tb, rb, ch, ob, s_ref, m_ref, va, vm,
-    loc, kvs, kvr, qs, qr, bs, br, rs, rr, gs, gr, os_, or_,
+    qb, kv, vt, tb, rb, ch, raw, ob, s_ref, m_ref, va, vm,
+    loc, kvs, kvr, qs, qr, bs, br, ws, wr, fs, fr,
+    rs, rr, gs, gr, os_, or_, rdy,
 ):
     c = lax.axis_index("ctx")
     h = lax.axis_index("head")
@@ -60,9 +61,9 @@
         pltpu.make_async_copy(ref, ref, sem).wait()
 
     def offset(i):
-        j = (i - 1) // 2
-        dy = jnp.where(i == 0, 0, jnp.where(i == 7, 0, 1 + 2 * j - 3 * (j // 2)))
-        dc = jnp.where(i == 0, 1, jnp.where(i == 7, 0, (i - 1) % 2))
+        r = i % 3
+        dy = jnp.where(i < 6, 2 - r + 3 * (r // 2), 0)
+        dc = jnp.where(i < 6, i // 3, 7 - i)
         return dy, dc
 
     def source(i):
@@ -94,23 +95,35 @@
     own_q.start()
 
     barrier = pltpu.get_barrier_semaphore()
+
+    def signal(sem, cc, hh):
+        pl.semaphore_signal(sem, inc=1, device_id={"ctx": cc, "head": hh},
+                            device_id_type=pl.DeviceIdType.MESH)
+
     for d in range(1, NH):
-        pl.semaphore_signal(barrier, inc=1, device_id={"ctx": c, "head": (h + d) % NH},
-                            device_id_type=pl.DeviceIdType.MESH)
-    for d in range(1, NC):
-        pl.semaphore_signal(barrier, inc=1, device_id={"ctx": (c + d) % NC, "head": h},
-                            device_id_type=pl.DeviceIdType.MESH)
+        signal(barrier, c, (h + d) % NH)
+    place_here = z * 4 + x
+    others = [(n, (n % 4) * 4 + n // 4) for n in range(NC)]
+    for n, place in others:
+        @pl.when(place > place_here)
+        def _():
+            signal(barrier, n, h)
     kv[pl.ds(BAND + SLAB, ROWS), :] = jnp.zeros((ROWS, 2 * DH), jnp.bfloat16)
-
-    @pl.when(c < 4)
-    def _():
-        vt[...] = jnp.zeros_like(vt)
-        for d in range(1, 5):
-            @pl.when(c < d)
-            def _():
-                kv[pl.ds((4 - d) * SLAB, SLAB), :] = jnp.zeros((SLAB, 2 * DH), jnp.bfloat16)
-
-    pl.semaphore_wait(barrier, NH - 1 + NC - 1)
+    for d in range(1, 5):
+        @pl.when(c < d)
+        def _():
+            kv[pl.ds((4 - d) * SLAB, SLAB), :] = jnp.zeros((SLAB, 2 * DH), jnp.bfloat16)
+
+    pl.semaphore_wait(barrier, NH - 1 + place_here)
+    for n, place in others:
+        @pl.when(place < place_here)
+        def _():
+            signal(rdy.at[c], n, h)
+
+    def ready(n):
+        @pl.when((n % 4) * 4 + n // 4 > place_here)
+        def _():
+            pl.semaphore_wait(rdy.at[n], 1)
 
     def kv_copies(i):
         t = target(i)
@@ -125,17 +138,39 @@
         return remote(q_hbm.at[:, pl.ds(pl.multiple_of(t * WIDTH, WIDTH), WIDTH)],
                       qb.at[h], qs.at[t], qr.at[h], c, t)
 
+    far = pl.ds(pl.multiple_of(h * ROWS, ROWS), ROWS)
+
+    def raw_copy(n):
+        return remote((k_hbm, v_hbm)[n], raw.at[n], ws.at[n], wr.at[n], c + 4, h)
+
+    def far_copies(i):
+        t = target(i)
+        return [
+            remote(raw.at[n, :, pl.ds(pl.multiple_of(t * DH, DH), DH)],
+                   kv.at[far, pl.ds(n * DH, DH)], fs.at[t], fr.at[h], c, t)
+            for n in range(2)
+        ]
+
     for i in range(7):
         for cp in kv_copies(i):
             cp.start()
-    for i in range(7):
-        q_copy(i).start()
+    q_copy(6).start()
+
+    @pl.when(x < 3)
+    def _():
+        pl.semaphore_wait(rdy.at[c + 4], 1)
+        for n in range(2):
+            raw_copy(n).start()
 
     own_k.wait()
     own_v.wait()
     for i in range(7):
         s = source(i)
         drain(kv.at[pl.ds(pl.multiple_of(BAND + s * ROWS, ROWS), ROWS), :], kvr.at[s])
+    for n in range(NC):
+        @pl.when(n != c + 4)
+        def _():
+            ready(n)
 
     def slab(d):
         return kv.at[pl.ds((4 - d) * SLAB, SLAB), :]
@@ -148,6 +183,12 @@
         def _():
             remote(piece(d_src, k), piece(d_dst, k), bs.at[n], br.at[d_dst - 1, k], cc, h).start()
 
+    def far_landed(k):
+        for e in (2 * k, 2 * k + 1):
+            @pl.when((c >= 4) & (h != e))
+            def _():
+                drain(kv.at[pl.ds(e * ROWS, ROWS), :], fr.at[e])
+
     def landed(d, k):
         @pl.when(c >= d)
         def _():
@@ -155,6 +196,13 @@
 
     middle = (z == 1) | (z == 2)
     back = x > 0
+
+    chunk = pl.ds(pl.multiple_of(c * ROWS, ROWS), ROWS)
+
+    def local(src, dst, sem):
+        cp = pltpu.make_async_copy(src, dst, sem)
+        cp.start()
+        return cp
 
     def table_send():
         @pl.when(x < 3)
@@ -163,38 +211,32 @@
                 place = pick((VW, 2 * DH), b) - 4 * c
                 tb[pl.ds(b * VW, VW), :] = choose(
                     [(place == n, kv[pl.ds(BAND + n * VW, VW), :]) for n in range(4)])
-            own = pltpu.make_async_copy(tb.at[pl.ds(pl.multiple_of(c * ROWS, ROWS), ROWS), :],
-                                        rb.at[c], loc.at[3])
-            own.start()
             for d in range(1, NC):
                 j = (c + d) % NC
                 remote(tb.at[pl.ds(pl.multiple_of(j * ROWS, ROWS), ROWS), :], rb.at[c],
                        rs.at[j], rr.at[c], j, h).start()
-            own.wait()
+            local(tb.at[chunk, :], rb.at[c], loc.at[3]).wait()
 
     def table_spread():
         for s in range(12):
             @pl.when(c != s)
             def _():
                 drain(rb.at[s], rr.at[s])
-        holder = pick((ROWS, 2 * DH), c // 2)
-        ch[...] = choose(
-            [((holder >= 4 * s) & (holder < 4 * s + 4), rb[s]) for s in range(12)])
+        r = rb[0].astype(jnp.float32)
+        for s in range(1, 12):
+            r = r + rb[s].astype(jnp.float32)
+        ch[...] = r.astype(jnp.bfloat16)
         for d in range(1, NC):
             j = (c + d) % NC
 
             @pl.when(j >= 4)
             def _():
-                remote(ch, vt.at[pl.ds(pl.multiple_of(c * ROWS, ROWS), ROWS), :],
-                       gs.at[j], gr.at[c], j, h).start()
+                remote(ch, vt.at[chunk, :], gs.at[j], gr.at[c], j, h).start()
 
     def table_wait():
         @pl.when(c >= 4)
         def _():
-            own = pltpu.make_async_copy(ch, vt.at[pl.ds(pl.multiple_of(c * ROWS, ROWS), ROWS), :],
-                                        loc.at[4])
-            own.start()
-            own.wait()
+            local(ch, vt.at[chunk, :], loc.at[4]).wait()
             for s in range(NC):
                 @pl.when(c != s)
                 def _():
@@ -202,12 +244,25 @@
 
     table_send()
     for k in range(NPIECE):
-        hop(2, x < 3, 0, 4, c + 4, k)
         hop(0, z < 3, 0, 1, c + 1, k)
         hop(1, z == 0, 0, 3, c + 3, k)
+
+    @pl.when(x > 0)
+    def _():
+        for n in range(2):
+            drain(raw.at[n], wr.at[n])
+        for i in range(7):
+            for cp in far_copies(i):
+                cp.start()
+        for n in range(2):
+            local(raw.at[n, :, pl.ds(pl.multiple_of(h * DH, DH), DH)],
+                  kv.at[far, pl.ds(n * DH, DH)], loc.at[6]).wait()
+
+    for i in range(6):
+        q_copy(i).start()
     table_spread()
     for k in range(NPIECE):
-        landed(4, k)
+        far_landed(k)
         hop(3, back & (z > 0), 4, 3, c - 1, k)
         hop(4, back & (z == 3), 4, 1, c - 3, k)
     for k in range(NPIECE):
@@ -348,12 +403,24 @@
             cp.wait_send()
         q_copy(i).wait_send()
     for n, cond, d in (
-        (0, z < 3, 0), (1, z == 0, 0), (2, x < 3, 0), (3, back & (z > 0), 4),
+        (0, z < 3, 0), (1, z == 0, 0), (3, back & (z > 0), 4),
         (4, back & (z == 3), 4), (5, middle, 1), (6, back & middle, 3),
     ):
         @pl.when(cond)
         def _():
             drain(slab(d), bs.at[n])
+
+    @pl.when(x < 3)
+    def _():
+        for n in range(2):
+            drain(raw.at[n], ws.at[n])
+
+    @pl.when(x > 0)
+    def _():
+        for i in range(7):
+            for cp in far_copies(i):
+                cp.wait_send()
+
     for d in range(1, NC):
         j = (c + d) % NC
 
@@ -387,14 +454,16 @@
             pltpu.VMEM((NVB * VW, 2 * DH), bf),
             pltpu.VMEM((12, ROWS, 2 * DH), bf),
             pltpu.VMEM((ROWS, 2 * DH), bf),
+            pltpu.VMEM((2, ROWS, NH * DH), bf),
             pltpu.VMEM((NH, ROWS, WIDTH), bf),
             pltpu.VMEM((2, M, NK), jnp.float32),
             pltpu.VMEM((2, M, VW), jnp.float32),
             pltpu.VMEM((NH, M, 2 * DH), jnp.float32),
             pltpu.VMEM((NH, M, VW), jnp.float32),
             dma((8,)), dma((NH,)), dma((NH,)), dma((NH,)), dma((NH,)),
-            dma((8,)), dma((4, NPIECE)), dma((NC,)), dma((12,)), dma((NC,)), dma((NC,)),
-            dma((NH,)), dma((NH,)),
+            dma((8,)), dma((4, NPIECE)), dma((2,)), dma((2,)), dma((NH,)), dma((NH,)),
+            dma((NC,)), dma((12,)), dma((NC,)), dma((NC,)), dma((NH,)), dma((NH,)),
+            pltpu.SemaphoreType.REGULAR((NC,)),
         ],
         compiler_params=pltpu.CompilerParams(
             collective_id=0, has_side_effects=True, vmem_limit_bytes=60 * 2**20),

time: 68.2 us -> 61.5 us (0.902); the launches traced: 68 us -> 60.3 us
  Pallas kernels: 65.8 us -> 58 us
    pallas_call x1, Pallas kernels: 65.8 us -> 58 us  [per_device(): pl.pallas_call(kernel, out_shape=jax.ShapeDtypeStruct((ROWS, NH * WIDTH),...]
where the time goes in v3:
time: 61.5 us; the launch traced here: 60.3 us
  Pallas kernels  58 us (94%)
  local copies, waits for them, and re-layouts  2.26 us (4%)
    pallas_call x1, Pallas kernels, per_device(): pl.pallas_call(kernel, out_shape=jax.ShapeDtypeStruct((ROWS, NH * WIDTH),...  58 us
    unnamed x1, local copies, waits for them, and re-layouts  2.26 us

profile of v3, /device:TPU:29, one launch (start us, length us, event | category | flops | bytes accessed | tf_op | source)
XLA Modules:
  0.0 60.3 jit_solution(4713103640503560840)
XLA Ops:
  0.0 58.0 %sparse_attention.1 = bf16[64,8192]{1,0:T(8,128)(2,1)} custom-call(bf16[64,8192]{1,0:T(8,128)(2,1)} %q_hbm.1, bf16[64,1024]{1,0:T(8,128)(2,1)} %k_hbm.1, bf16[64,1024]{1,0:T(8,128)(2,1)} %v_hbm.1, s32[1,8]{1,0:T(1,128)} %vb_ref.1), custom_call_target="tpu_custom_call" | custom-call | tf_op jit(solution)/shard_map/sparse_attention/pallas_call | solution.py:445
  58.0 2.3 %copy.6 = bf16[64,8192]{1,0:T(8,128)(2,1)} copy(bf16[64,8192]{1,0:T(8,128)(2,1)} %sparse_attention.1) | data formatting | bytes 2097152

commit v4 on v2

v4 whole, which is shorter than its diff:
```python
import functools
import math

import jax
import jax.numpy as jnp
from jax import lax
from jax.experimental import pallas as pl
from jax.experimental.pallas import tpu as pltpu
from jax.sharding import PartitionSpec as P

DH = 128
VW = 128
NVB = 8
NC = 16
NH = 8
ROWS = 64
SLAB = 512
BAND = 2048
HPG = 8
WIDTH = HPG * DH
M = ROWS * HPG
NEARK = SLAB + 2 * ROWS
NEARROWS = 2 * SLAB + ROWS
MIDK = 3 * SLAB
RESTK = MIDK + NVB * VW
KB = 256
PIECE = 128
NPIECE = SLAB // PIECE
QUART = 256
NEG = -1e30
SCALE = math.log2(math.e) / math.sqrt(float(DH))

def cut(kind, size, col):
    return [(kind, o, min(KB, size - o), col + o) for o in range(0, size, KB)]


NEAR = cut(0, NEARK, 0)
REST = cut(1, MIDK, 0) + cut(2, NVB * VW, MIDK)


def kernel(
    q_hbm, k_hbm, v_hbm, vb_ref, out_hbm,
    qb, near, mid, vt, tb, rb, ub, zb, ch, ob, s_ref, m_ref, va, vm,
    loc, kvs, kvr, qs, qr, bs, br,
    sxs, sxr, szs, szr, gzs, gzr, gxs, gxr, os_, or_, rx, rz,
):
    c = lax.axis_index("ctx")
    h = lax.axis_index("head")
    x = c // 4
    z = c % 4
    y = h // 2
    core = h % 2

    def remote(src, dst, ssem, rsem, cc, hh):
        return pltpu.make_async_remote_copy(
            src_ref=src, dst_ref=dst, send_sem=ssem, recv_sem=rsem,
            device_id={"ctx": cc, "head": hh}, device_id_type=pl.DeviceIdType.MESH,
        )

    def drain(ref, sem):
        pltpu.make_async_copy(ref, ref, sem).wait()

    def offset(i):
        r = i % 3
        dy = jnp.where(i < 6, 2 - r + 3 * (r // 2), 0)
        dc = jnp.where(i < 6, i // 3, 7 - i)
        return dy, dc

    def source(i):
        dy, dc = offset(i)
        return ((y + dy) % 4) * 2 + (core + dc) % 2

    def target(i):
        dy, dc = offset(i)
        return ((y + 4 - dy) % 4) * 2 + (core + 2 - dc) % 2

    def pick(shape, b):
        return jnp.zeros(shape, jnp.int32) + vb_ref[0, b]

    def choose(cases):
        r = jnp.zeros(cases[0][1].shape, jnp.float32)
        for mask, value in cases:
            r = jnp.where(mask, value.astype(jnp.float32), r)
        return r.astype(jnp.bfloat16)

    mine = pl.ds(pl.multiple_of(SLAB + h * ROWS, ROWS), ROWS)
    own_k = pltpu.make_async_copy(
        k_hbm.at[:, pl.ds(pl.multiple_of(h * DH, DH), DH)], near.at[mine, pl.ds(0, DH)], loc.at[0])
    own_v = pltpu.make_async_copy(
        v_hbm.at[:, pl.ds(pl.multiple_of(h * DH, DH), DH)], near.at[mine, pl.ds(DH, DH)], loc.at[1])
    own_q = pltpu.make_async_copy(
        q_hbm.at[:, pl.ds(pl.multiple_of(h * WIDTH, WIDTH), WIDTH)], qb.at[h], loc.at[2])
    own_k.start()
    own_v.start()
    own_q.start()

    barrier = pltpu.get_barrier_semaphore()

    def at(xx, zz):
        return xx * 4 + zz

    def signal(sem, cc, hh):
        pl.semaphore_signal(sem, inc=1, device_id={"ctx": cc, "head": hh},
                            device_id_type=pl.DeviceIdType.MESH)

    for d in range(1, NH):
        signal(barrier, c, (h + d) % NH)
    for n in range(1, 4):
        @pl.when(n > x)
        def _():
            signal(barrier, at(n, z), h)

        @pl.when(n > z)
        def _():
            signal(barrier, at(x, n), h)
    near[pl.ds(2 * SLAB, ROWS), :] = jnp.zeros((ROWS, 2 * DH), jnp.bfloat16)

    @pl.when(c < 4)
    def _():
        near[pl.ds(0, SLAB), :] = jnp.zeros((SLAB, 2 * DH), jnp.bfloat16)
        vt[...] = jnp.zeros_like(vt)
        for d in range(1, 4):
            @pl.when(c < d)
            def _():
                mid[pl.ds((3 - d) * SLAB, SLAB), :] = jnp.zeros((SLAB, 2 * DH), jnp.bfloat16)

    pl.semaphore_wait(barrier, NH - 1 + x + z)
    for n in range(3):
        @pl.when(n < x)
        def _():
            signal(rx.at[x], at(n, z), h)

        @pl.when(n < z)
        def _():
            signal(rz.at[z], at(x, n), h)

    def kv_copies(i):
        t = target(i)
        return [
            remote(src.at[:, pl.ds(pl.multiple_of(t * DH, DH), DH)],
                   near.at[mine, pl.ds(n * DH, DH)], kvs.at[t], kvr.at[h], c, t)
            for n, src in enumerate((k_hbm, v_hbm))
        ]

    def q_copy(i):
        t = target(i)
        return remote(q_hbm.at[:, pl.ds(pl.multiple_of(t * WIDTH, WIDTH), WIDTH)],
                      qb.at[h], qs.at[t], qr.at[h], c, t)

    for i in range(7):
        for cp in kv_copies(i):
            cp.start()
    q_copy(6).start()

    for i in range(6):
        q_copy(i).start()
    own_k.wait()
    own_v.wait()
    for i in range(7):
        s = source(i)
        drain(near.at[pl.ds(pl.multiple_of(SLAB + s * ROWS, ROWS), ROWS), :], kvr.at[s])
    for n in range(1, 4):
        @pl.when(n > x)
        def _():
            pl.semaphore_wait(rx.at[n], 1)

        @pl.when(n > z)
        def _():
            pl.semaphore_wait(rz.at[n], 1)

    def part(d, start, rows):
        if d == 0 or d == 4:
            return near.at[pl.ds(start + (SLAB if d == 0 else 0), rows), :]
        return mid.at[pl.ds(start + (3 - d) * SLAB, rows), :]

    def slab(d):
        return part(d, 0, SLAB)

    def piece(d, k):
        return part(d, k * PIECE, PIECE)

    def hop(n, cond, d_src, d_dst, cc, k):
        @pl.when(cond)
        def _():
            remote(piece(d_src, k), piece(d_dst, k), bs.at[n], br.at[d_dst - 1, k], cc, h).start()

    def landed(d, k):
        @pl.when(c >= d)
        def _():
            drain(piece(d, k), br.at[d - 1, k])

    middle = (z == 1) | (z == 2)
    back = x > 0

    quarter = pl.ds(pl.multiple_of(x * QUART, QUART), QUART)
    chunk = pl.ds(pl.multiple_of(x * QUART + z * ROWS, ROWS), ROWS)

    def local(src, dst, sem):
        cp = pltpu.make_async_copy(src, dst, sem)
        cp.start()
        return cp

    def total(parts):
        r = parts[0].astype(jnp.float32)
        for e in parts[1:]:
            r = r + e.astype(jnp.float32)
        return r.astype(jnp.bfloat16)

    def table_add_x():
        @pl.when(x < 3)
        def _():
            for b in range(NVB):
                place = pick((VW, 2 * DH), b) - 4 * c
                tb[pl.ds(b * VW, VW), :] = choose(
                    [(place == n, near[pl.ds(SLAB + n * VW, VW), :]) for n in range(4)])
            for n in range(4):
                @pl.when(n != x)
                def _():
                    remote(tb.at[pl.ds(n * QUART, QUART), :], rb.at[x],
                           sxs.at[n], sxr.at[x], at(n, z), h).start()
            local(tb.at[quarter, :], rb.at[x], loc.at[3]).wait()

    def table_add_z():
        for n in range(3):
            @pl.when(n != x)
            def _():
                drain(rb.at[n], sxr.at[n])
        ub[...] = total([rb[n] for n in range(3)])
        for n in range(4):
            @pl.when(n != z)
            def _():
                remote(ub.at[pl.ds(n * ROWS, ROWS), :], zb.at[z],
                       szs.at[n], szr.at[z], at(x, n), h).start()
        local(ub.at[pl.ds(pl.multiple_of(z * ROWS, ROWS), ROWS), :], zb.at[z], loc.at[3]).wait()

    def table_gather_z():
        for n in range(4):
            @pl.when(n != z)
            def _():
                drain(zb.at[n], szr.at[n])
        ch[...] = total([zb[n] for n in range(4)])
        for n in range(4):
            @pl.when(n != z)
            def _():
                remote(ch, vt.at[chunk, :], gzs.at[n], gzr.at[z], at(x, n), h).start()
        local(ch, vt.at[chunk, :], loc.at[4]).wait()

    def table_gather_x():
        for n in range(4):
            @pl.when(n != z)
            def _():
                drain(ch, gzr.at[n])
        for n in range(1, 4):
            @pl.when(n != x)
            def _():
                remote(vt.at[quarter, :], vt.at[quarter, :],
                       gxs.at[n], gxr.at[x], at(n, z), h).start()

    def table_wait():
        for n in range(4):
            @pl.when((x > 0) & (n != x))
            def _():
                drain(vt.at[pl.ds(n * QUART, QUART), :], gxr.at[n])

    table_add_x()
    for k in range(NPIECE):
        hop(2, x < 3, 0, 4, c + 4, k)
    for k in range(NPIECE):
        hop(0, z < 3, 0, 1, c + 1, k)
        hop(1, z == 0, 0, 3, c + 3, k)
    table_add_z()
    for k in range(NPIECE):
        landed(4, k)
        hop(3, back & (z > 0), 4, 3, c - 1, k)
        hop(4, back & (z == 3), 4, 1, c - 3, k)
    table_gather_z()
    for k in range(NPIECE):
        landed(1, k)
        hop(5, middle, 1, 2, c + 1, k)
    table_gather_x()
    for k in range(NPIECE):
        landed(3, k)
        hop(6, back & middle, 3, 2, c - 1, k)

    ii = lax.broadcasted_iota(jnp.int32, (ROWS, VW), 0)
    jj = lax.broadcasted_iota(jnp.int32, (ROWS, VW), 1)
    missing = (jnp.where(c < 4, SLAB, 0), jnp.maximum(3 - c, 0) * SLAB)

    def keep(mask, t):
        return jnp.where(mask[None], t.reshape(HPG, ROWS, VW), NEG).reshape(M, VW)

    def load_q(p):
        return jnp.concatenate([qb[p, :, n * DH:(n + 1) * DH] for n in range(HPG)], axis=0)

    def load(p, blk, column):
        kind, off, w, _ = blk
        cols = pl.ds(column * DH, DH)
        if kind == 0:
            return near[pl.ds(pl.multiple_of(p * ROWS, ROWS) + off, w), cols]
        return mid[pl.ds(off, w), cols] if kind == 1 else vt[pl.ds(off, w), cols]

    def scores(p, q, blk, slot, mx):
        kind, off, w, col = blk
        k = load(p, blk, 0)
        s = lax.dot_general(q, k, (((1,), (1,)), ((), ())), preferred_element_type=jnp.float32)
        for t in range(w // VW):
            e = s[:, t * VW:(t + 1) * VW]
            o = off + t * VW
            if kind == 0:
                mask = jj >= missing[0] - p * ROWS - o
                if o == 0:
                    mask = mask & (jj > ii)
                if o + VW == NEARK:
                    mask = mask & (jj <= ii)
            elif kind == 1:
                mask = jj >= missing[1] - o
            else:
                mask = (jj - ii + pick((ROWS, VW), o // VW) * VW) <= (c * SLAB + p * ROWS - BAND)
            e = keep(mask, e)
            mx = e if mx is None else jnp.maximum(mx, e)
            s_ref[slot, :, col + t * VW:col + (t + 1) * VW] = e
        return mx

    def row_max(mx):
        return jnp.broadcast_to(jnp.max(mx, axis=1, keepdims=True) * SCALE, (M, VW))

    def weigh(p, blk, slot, acc):
        kind, off, w, col = blk
        v = load(p, blk, 1)
        v = jnp.concatenate([v, jnp.ones((w, DH), jnp.bfloat16)], axis=1)
        m = m_ref[slot]
        e = [jnp.exp2(s_ref[slot, :, col + t * VW:col + (t + 1) * VW] * SCALE - m).astype(jnp.bfloat16)
             for t in range(w // VW)]
        d = jnp.dot(jnp.concatenate(e, axis=1), v, preferred_element_type=jnp.float32)
        return d if acc is None else acc + d

    def out_copy(p):
        return remote(ob.at[p], out_hbm.at[:, pl.ds(pl.multiple_of(h * WIDTH, WIDTH), WIDTH)],
                      os_.at[p], or_.at[h], c, p)

    def unit_loop(blocks, before, top, after):
        def begin(i):
            before(i)
            return source(i)

        def stage(i, slot):
            p = source(i)
            n = begin(jnp.minimum(i + 1, 7))
            q = load_q(n)
            acc = mx = None
            for blk in blocks:
                mx = scores(n, q, blk, 1 - slot, mx)
                acc = weigh(p, blk, slot, acc)
            after(i, p, slot, acc)
            m_ref[1 - slot] = top(n, row_max(mx))

        n = begin(0)
        q = load_q(n)
        mx = None
        for blk in blocks:
            mx = scores(n, q, blk, 0, mx)
        m_ref[0] = top(n, row_max(mx))

        def body(t, carry):
            stage(2 * t, 0)
            stage(2 * t + 1, 1)
            return carry

        lax.fori_loop(0, 4, body, 0)

    own_q.wait()

    def q_arrived(i):
        @pl.when(i < 7)
        def _():
            n = source(i)
            drain(qb.at[n], qr.at[n])

    def keep_near(i, p, slot, acc):
        va[p] = acc
        vm[p] = m_ref[slot]

    unit_loop(NEAR, q_arrived, lambda n, m: m, keep_near)

    for k in range(NPIECE):
        landed(2, k)
    table_wait()

    def finish(i, p, slot, acc):
        f = jnp.exp2(vm[p] - m_ref[slot])
        acc = acc + va[p] * jnp.concatenate([f, f], axis=1)
        o = (acc[:, :DH] / acc[:, DH:]).astype(jnp.bfloat16)
        for t in range(HPG):
            ob[p, :, t * DH:(t + 1) * DH] = o[t * ROWS:(t + 1) * ROWS]

        @pl.when(i < 7)
        def _():
            out_copy(p).start()

    unit_loop(REST, lambda i: None, lambda n, m: jnp.maximum(m, vm[n]), finish)

    own_o = pltpu.make_async_copy(
        ob.at[h], out_hbm.at[:, pl.ds(pl.multiple_of(h * WIDTH, WIDTH), WIDTH)], loc.at[5])
    own_o.start()

    for i in range(7):
        t = target(i)
        for cp in kv_copies(i):
            cp.wait_send()
        q_copy(i).wait_send()
    for n, cond, d in (
        (0, z < 3, 0), (1, z == 0, 0), (2, x < 3, 0), (3, back & (z > 0), 4),
        (4, back & (z == 3), 4), (5, middle, 1), (6, back & middle, 3),
    ):
        @pl.when(cond)
        def _():
            drain(slab(d), bs.at[n])

    for n in range(4):
        @pl.when((x < 3) & (n != x))
        def _():
            drain(rb.at[0], sxs.at[n])

        @pl.when(n != z)
        def _():
            drain(ch, szs.at[n])
            drain(ch, gzs.at[n])

        if n > 0:
            @pl.when(n != x)
            def _():
                drain(rb.at[0], gxs.at[n])
    for i in range(7):
        p = source(i)
        drain(ob.at[p], os_.at[p])
        drain(out_hbm.at[:, pl.ds(pl.multiple_of(p * WIDTH, WIDTH), WIDTH)], or_.at[p])
    own_o.wait()


def per_device(queries, keys, values, vert_blocks):
    anywhere = pl.BlockSpec(memory_space=pl.ANY)
    queries, keys, values, vert_blocks = (
        pltpu.with_memory_space_constraint(e, pltpu.HBM)
        for e in (queries, keys, values, vert_blocks))
    dma = pltpu.SemaphoreType.DMA
    bf = jnp.bfloat16
    return pl.pallas_call(
        kernel,
        out_shape=jax.ShapeDtypeStruct((ROWS, NH * WIDTH), bf),
        in_specs=[anywhere, anywhere, anywhere, pl.BlockSpec(memory_space=pltpu.SMEM)],
        out_specs=anywhere,
        scratch_shapes=[
            pltpu.VMEM((NH, ROWS, WIDTH), bf),
            pltpu.VMEM((NEARROWS, 2 * DH), bf),
            pltpu.VMEM((MIDK, 2 * DH), bf),
            pltpu.VMEM((NVB * VW, 2 * DH), bf),
            pltpu.VMEM((NVB * VW, 2 * DH), bf),
            pltpu.VMEM((3, QUART, 2 * DH), bf),
            pltpu.VMEM((QUART, 2 * DH), bf),
            pltpu.VMEM((4, ROWS, 2 * DH), bf),
            pltpu.VMEM((ROWS, 2 * DH), bf),
            pltpu.VMEM((NH, ROWS, WIDTH), bf),
            pltpu.VMEM((2, M, RESTK), jnp.float32),
            pltpu.VMEM((2, M, VW), jnp.float32),
            pltpu.VMEM((NH, M, 2 * DH), jnp.float32),
            pltpu.VMEM((NH, M, VW), jnp.float32),
            dma((8,)), dma((NH,)), dma((NH,)), dma((NH,)), dma((NH,)),
            dma((8,)), dma((4, NPIECE)), *[dma((4,)) for _ in range(8)], dma((NH,)), dma((NH,)),
            pltpu.SemaphoreType.REGULAR((4,)), pltpu.SemaphoreType.REGULAR((4,)),
        ],
        compiler_params=pltpu.CompilerParams(
            collective_id=0, has_side_effects=True, vmem_limit_bytes=32 * 2**20),
        name="sparse_attention",
    )(queries, keys, values, vert_blocks)


def solution(mesh):
    placed = (
        P(("ctx", "head"), None),
        P(("ctx", "head"), None),
        P(("ctx", "head"), None),
        P("head", None),
    )
    return jax.shard_map(
        per_device, mesh=mesh, in_specs=placed, out_specs=P(("ctx", "head"), None), check_vma=False
    )
```

time: 68.2 us -> 56.4 us (0.83)
  Pallas kernels: 65.8 us -> 54.8 us
  local copies, waits for them, and re-layouts: 2.26 us -> 0.97 us
    pallas_call x1, Pallas kernels: 65.8 us -> 54.8 us  [per_device(): pl.pallas_call(kernel, out_shape=jax.ShapeDtypeStruct((ROWS, NH * WIDTH),...]
    unnamed x1, local copies, waits for them, and re-layouts: 2.26 us -> 0.97 us
where the time goes in v4:
time: 56.4 us; the launch traced here: 55.8 us
  Pallas kernels  54.8 us (97%)
  local copies, waits for them, and re-layouts  0.97 us (2%)
    pallas_call x1, Pallas kernels, per_device(): pl.pallas_call(kernel, out_shape=jax.ShapeDtypeStruct((ROWS, NH * WIDTH),...  54.8 us

profile of v4, /device:TPU:29, one launch (start us, length us, event | category | flops | bytes accessed | tf_op | source)
XLA Modules:
  0.0 55.8 jit_solution(834931231283739306)
XLA Ops:
  0.0 54.8 %sparse_attention.1 = bf16[64,8192]{1,0:T(8,128)(2,1)S(1)} custom-call(bf16[64,8192]{1,0:T(8,128)(2,1)} %q_hbm.1, bf16[64,1024]{1,0:T(8,128)(2,1)} %k_hbm.1, bf16[64,1024]{1,0:T(8,128)(2,1)} %v_hbm.1, s32[1,8]{1,0:T(1,128)} %vb_ref.1), custom_call_target="tpu_custom_call" | custom-call | tf_op jit(solution)/shard_map/sparse_attention/pallas_call | solution.py:447
  54.8 1.0 %copy.6 = bf16[64,8192]{1,0:T(8,128)(2,1)} copy(bf16[64,8192]{1,0:T(8,128)(2,1)S(1)} %sparse_attention.1) | data formatting | bytes 2097152

commit v5 on v4

--- a/solution.py
+++ b/solution.py
@@ -243,18 +243,22 @@
             @pl.when(n != z)
             def _():
                 remote(ch, vt.at[chunk, :], gzs.at[n], gzr.at[z], at(x, n), h).start()
+        table_across(ch, chunk)
         local(ch, vt.at[chunk, :], loc.at[4]).wait()
+
+    def table_across(src, rows):
+        for n in range(1, 4):
+            @pl.when(n != x)
+            def _():
+                remote(src, vt.at[rows, :], gxs.at[n], gxr.at[x], at(n, z), h).start()
 
     def table_gather_x():
         for n in range(4):
             @pl.when(n != z)
             def _():
                 drain(ch, gzr.at[n])
-        for n in range(1, 4):
-            @pl.when(n != x)
-            def _():
-                remote(vt.at[quarter, :], vt.at[quarter, :],
-                       gxs.at[n], gxr.at[x], at(n, z), h).start()
+                rows = pl.ds(pl.multiple_of(x * QUART + n * ROWS, ROWS), ROWS)
+                table_across(vt.at[rows, :], rows)
 
     def table_wait():
         for n in range(4):

time: 56.4 us -> 56.4 us (level)
  no operation moved by 1% of the time
where the time goes in v5:
time: 56.4 us; the launch traced here: 55.7 us
  Pallas kernels  54.7 us (97%)
  local copies, waits for them, and re-layouts  0.97 us (2%)
    pallas_call x1, Pallas kernels, per_device(): pl.pallas_call(kernel, out_shape=jax.ShapeDtypeStruct((ROWS, NH * WIDTH),...  54.7 us

profile of v5, /device:TPU:29, one launch (start us, length us, event | category | flops | bytes accessed | tf_op | source)
XLA Modules:
  0.0 55.7 jit_solution(16642868306166534665)
XLA Ops:
  0.0 54.7 %sparse_attention.1 = bf16[64,8192]{1,0:T(8,128)(2,1)S(1)} custom-call(bf16[64,8192]{1,0:T(8,128)(2,1)} %q_hbm.1, bf16[64,1024]{1,0:T(8,128)(2,1)} %k_hbm.1, bf16[64,1024]{1,0:T(8,128)(2,1)} %v_hbm.1, s32[1,8]{1,0:T(1,128)} %vb_ref.1), custom_call_target="tpu_custom_call" | custom-call | tf_op jit(solution)/shard_map/sparse_attention/pallas_call | solution.py:451
  54.7 1.0 %copy.6 = bf16[64,8192]{1,0:T(8,128)(2,1)} copy(bf16[64,8192]{1,0:T(8,128)(2,1)S(1)} %sparse_attention.1) | data formatting | bytes 2097152

commit v6 on v5

--- a/solution.py
+++ b/solution.py
@@ -362,6 +362,8 @@
         q = load_q(n)
         mx = None
         for blk in blocks:
+            if blk[0] == 2 and blk[1] == 0:
+                table_wait()
             mx = scores(n, q, blk, 0, mx)
         m_ref[0] = top(n, row_max(mx))
 
@@ -388,7 +390,6 @@
 
     for k in range(NPIECE):
         landed(2, k)
-    table_wait()
 
     def finish(i, p, slot, acc):
         f = jnp.exp2(vm[p] - m_ref[slot])

time: 56.4 us -> 56.6 us (level)
  no operation moved by 1% of the time
where the time goes in v6:
time: 56.6 us; the launch traced here: 55.8 us
  Pallas kernels  54.8 us (97%)
  local copies, waits for them, and re-layouts  0.97 us (2%)
    pallas_call x1, Pallas kernels, per_device(): pl.pallas_call(kernel, out_shape=jax.ShapeDtypeStruct((ROWS, NH * WIDTH),...  54.8 us

profile of v6, /device:TPU:29, one launch (start us, length us, event | category | flops | bytes accessed | tf_op | source)
XLA Modules:
  0.0 55.8 jit_solution(10166046556552618257)
XLA Ops:
  0.0 54.8 %sparse_attention.1 = bf16[64,8192]{1,0:T(8,128)(2,1)S(1)} custom-call(bf16[64,8192]{1,0:T(8,128)(2,1)} %q_hbm.1, bf16[64,1024]{1,0:T(8,128)(2,1)} %k_hbm.1, bf16[64,1024]{1,0:T(8,128)(2,1)} %v_hbm.1, s32[1,8]{1,0:T(1,128)} %vb_ref.1), custom_call_target="tpu_custom_call" | custom-call | tf_op jit(solution)/shard_map/sparse_attention/pallas_call | solution.py:452
  54.8 1.0 %copy.6 = bf16[64,8192]{1,0:T(8,128)(2,1)} copy(bf16[64,8192]{1,0:T(8,128)(2,1)S(1)} %sparse_attention.1) | data formatting | bytes 2097152

commit v7 on v5

--- a/solution.py
+++ b/solution.py
@@ -269,10 +269,10 @@
     table_add_x()
     for k in range(NPIECE):
         hop(2, x < 3, 0, 4, c + 4, k)
+    table_add_z()
     for k in range(NPIECE):
         hop(0, z < 3, 0, 1, c + 1, k)
         hop(1, z == 0, 0, 3, c + 3, k)
-    table_add_z()
     for k in range(NPIECE):
         landed(4, k)
         hop(3, back & (z > 0), 4, 3, c - 1, k)

time: 56.4 us -> 56.5 us (level)
  no operation moved by 1% of the time
where the time goes in v7:
time: 56.5 us; the launch traced here: 55.6 us
  Pallas kernels  54.6 us (97%)
  local copies, waits for them, and re-layouts  0.97 us (2%)
    pallas_call x1, Pallas kernels, per_device(): pl.pallas_call(kernel, out_shape=jax.ShapeDtypeStruct((ROWS, NH * WIDTH),...  54.6 us

profile of v7, /device:TPU:29, one launch (start us, length us, event | category | flops | bytes accessed | tf_op | source)
XLA Modules:
  0.0 55.6 jit_solution(5475513913296060816)
XLA Ops:
  0.0 54.6 %sparse_attention.1 = bf16[64,8192]{1,0:T(8,128)(2,1)S(1)} custom-call(bf16[64,8192]{1,0:T(8,128)(2,1)} %q_hbm.1, bf16[64,1024]{1,0:T(8,128)(2,1)} %k_hbm.1, bf16[64,1024]{1,0:T(8,128)(2,1)} %v_hbm.1, s32[1,8]{1,0:T(1,128)} %vb_ref.1), custom_call_target="tpu_custom_call" | custom-call | tf_op jit(solution)/shard_map/sparse_attention/pallas_call | solution.py:451
  54.6 1.0 %copy.6 = bf16[64,8192]{1,0:T(8,128)(2,1)} copy(bf16[64,8192]{1,0:T(8,128)(2,1)S(1)} %sparse_attention.1) | data formatting | bytes 2097152
